TPU v7x, 128 devices: a whole 4x4x4 slice. The times are simulated.
128 devices in a mesh: rep: 16 (over x, y), exp: 8 (over z, core).
Axes of the slice: x: 4, y: 4, z: 4, core: 2. Of those that a mesh axis runs over, the one named last changes fastest.
Arguments:
- hidden: bfloat16 [16384, 4096], P(('rep', 'exp')), may hold values from -6 to 6
- parents: int32 [16384], P(('rep', 'exp')), may hold values from 0 to 1023
- routes: int32 [16384, 8], P(('rep', 'exp')), may hold values from 0 to 127, all different within a row; in each aligned block of 128 rows (0 to 127, 128 to 255, ...) at most 10 rows name the same one
- gates: float32 [16384, 8], P(('rep', 'exp')), may hold values from 0.05 to 1
- counts: int32 [128], P(('rep', 'exp')), may hold values from 64 to 128, as said below
- norm_gain: float32 [4096], replicated, may hold values from 0.1 to 1.9
- w_gate: bfloat16 [128, 4096, 768], P(('rep', 'exp')), may hold values from -0.09375 to 0.09375
- w_up: bfloat16 [128, 4096, 768], P(('rep', 'exp')), may hold values from -0.09375 to 0.09375
- w_down: bfloat16 [128, 768, 4096], P(('rep', 'exp')), may hold values from -0.21875 to 0.21875
Outputs:
- mixed: bfloat16 [16384, 4096], P(('rep', 'exp'))
Inputs may be any that keep to these rules, and one draw needn't show every extreme that they name: `routes`: in the rows of one device no expert is named more than 10 times. `counts`: some device has all of its rows live.
All inputs are finite; a program needn't handle non-finite values.
Results may differ from a plain program's by a relative error of at most 0.0071.
Values may be sent and summed in bfloat16 or wider, within the bound.
A program may use at most 128 MiB of HBM per device.

v0:
```python
import jax
import jax.numpy as jnp
from jax import lax
from jax.sharding import PartitionSpec as P


def run_expert(arrived, w_gate, w_up, w_down):
    gate_val = jnp.dot(arrived, w_gate[0], preferred_element_type=jnp.float32)
    up_val = jnp.dot(arrived, w_up[0], preferred_element_type=jnp.float32)
    act = (jax.nn.silu(gate_val) * up_val).astype(jnp.bfloat16)
    return jnp.dot(act, w_down[0], preferred_element_type=jnp.float32).astype(jnp.bfloat16)


def shards(hidden, parents, routes, gates, counts, norm_gain, w_gate, w_up, w_down):
    rows = hidden.shape[0]
    width = hidden.shape[1]
    top = routes.shape[1]
    n_rep = lax.axis_size("rep")
    n_exp = lax.axis_size("exp")
    n_dev = n_rep * n_exp
    cap = rows * top // n_dev + 2
    column = lax.axis_index("exp")
    micro = rows * n_exp
    per_expert = cap * n_exp
    slots = n_rep * per_expert
    live = jnp.arange(rows, dtype=jnp.int32) < counts[0]
    weights = gates / jnp.sum(gates, axis=1, keepdims=True) * live[:, None].astype(jnp.float32)
    flat = routes.reshape(-1)
    live_slot = jnp.repeat(live, top)
    onehot = (
        (flat[:, None] == jnp.arange(n_dev, dtype=jnp.int32)[None, :]) & live_slot[:, None]
    ).astype(jnp.int32)
    before = jnp.cumsum(onehot, axis=0) - onehot
    rank = jnp.sum(before * onehot, axis=1)
    code = jnp.where(live_slot, flat, -1)
    ints = jnp.concatenate(
        [code.reshape(rows, top), rank.reshape(rows, top), parents[:, None]], axis=1
    )
    group = lax.all_gather(hidden, "exp", axis=0, tiled=True)
    ints_all = lax.all_gather(ints, "exp", axis=0, tiled=True)
    w_all = lax.all_gather(weights, "exp", axis=0, tiled=True)
    code_all = ints_all[:, :top]
    rank_all = ints_all[:, top : 2 * top]
    parent_all = ints_all[:, 2 * top]
    mine = (code_all >= 0) & (code_all % n_exp == column)
    owner = (jnp.arange(micro, dtype=jnp.int32) // rows)[:, None]
    dest = code_all // n_exp * per_expert + owner * cap + rank_all
    dest = jnp.where(mine, dest, slots).reshape(-1)
    row_id = jnp.broadcast_to(jnp.arange(micro, dtype=jnp.int32)[:, None], (micro, top)).reshape(-1)
    src_row = jnp.zeros((slots,), jnp.int32).at[dest].set(row_id, mode="drop")
    filled = jnp.zeros((slots,), jnp.bool_).at[dest].set(True, mode="drop")
    slot_w = jnp.zeros((slots,), jnp.float32).at[dest].set(w_all.reshape(-1), mode="drop")
    picked = jnp.take(group, jnp.take(parent_all, src_row), axis=0).astype(jnp.float32)
    scale = lax.rsqrt(jnp.mean(picked * picked, axis=1, keepdims=True) + 1e-06)
    normed = (picked * scale * norm_gain).astype(jnp.bfloat16)
    outgoing = jnp.where(filled[:, None], normed, jnp.zeros((), jnp.bfloat16))
    arrived = lax.all_to_all(outgoing, "rep", split_axis=0, concat_axis=0, tiled=True)
    results = run_expert(arrived, w_gate, w_up, w_down)
    returned = lax.all_to_all(results, "rep", split_axis=0, concat_axis=0, tiled=True)
    contrib = slot_w[:, None] * returned.astype(jnp.float32)
    target = jnp.where(filled, src_row, micro)
    partial = jnp.zeros((micro, width), jnp.float32).at[target].add(contrib, mode="drop")
    mixed = lax.psum_scatter(partial.astype(jnp.bfloat16), "exp", scatter_dimension=0, tiled=True)
    return mixed


def solution(mesh):
    placed = (
        P(("rep", "exp"), None),
        P(("rep", "exp")),
        P(("rep", "exp"), None),
        P(("rep", "exp"), None),
        P(("rep", "exp")),
        P(),
        P(("rep", "exp"), None, None),
        P(("rep", "exp"), None, None),
        P(("rep", "exp"), None, None),
    )
    return jax.shard_map(
        shards, mesh=mesh, in_specs=placed, out_specs=P(("rep", "exp"), None), check_vma=False
    )
```

profile of v0, /device:TPU:1, one launch (start us, length us, event | category | flops | bytes accessed | tf_op | source)
XLA Modules:
  0.0 590.4 jit_solution(2126128571061677138)
XLA Ops:
  6.5 0.0 all-gather.2.cloned.1.call-start
  6.5 0.7 all-gather.2.cloned.1.call-update
  7.3 0.8 copy.28
  8.0 0.1 eq.37
  8.1 0.1 eq.33
  8.9 0.1 broadcast_in_dim.94.clone
  9.0 0.1 and.55
  9.1 0.1 copy.31
  9.2 0.3 fusion.17
  9.7 0.1 copy.32
  9.8 0.5 fusion.16
  10.3 0.1 reshape.149
  10.4 0.7 broadcast_select_fusion
  11.1 0.7 pad_add_fusion
  11.8 15.3 %all_gather.9 = s32[1024,17]{0,1:T(8,128)S(1)} all-gather(s32[128,17]{0,1:T(8,128)S(1)} %pad_add_fusion), channel_id=1, replica_groups=mesh['rep'=16,'exp'=8] {'exp'}, dimensions={0}, use_global_device_ids=true | all-gather | bytes 78336 | tf_op jit(solution)/shard_map/all_gather | solution.py:40
  27.1 0.2 copy.34
  27.3 0.3 reshape.150
  27.7 34.6 %scatter_custom_fusion = pred[1280]{0:T(1024)(128)(4,1)S(1)} fusion(s32[8192]{0:T(1024)S(1)} %bitcast.48, pred[8192]{0:T(1024)(128)(4,1)S(1)} %broadcast.149, pred[]{:T(512)} %constant.90.clone.1), kind=kCustom, calls=%fused_computation.72 | custom fusion | bytes 1281 | tf_op jit(solution)/shard_map/scatter | solution.py:51
  62.3 0.1 broadcast_in_dim.105
  62.4 0.3 reshape.182
  62.7 30.9 %scatter_custom_fusion.1 = s32[1280]{0:T(1024)S(1)} fusion(s32[8192]{0:T(1024)S(1)} %bitcast.49, s32[8192]{0:T(1024)S(1)} %reshape.182, s32[]{:T(128)} %constant.93.clone.1), kind=kCustom, calls=%fused_computation.69 | custom fusion | bytes 5124 | tf_op jit(solution)/shard_map/scatter | solution.py:50
  93.6 5.0 gather_fusion
  98.6 0.1 broadcast_in_dim.109
  98.7 0.0 all-gather.2.cloned.1.call-done
  98.7 23.2 %gather_fusion.1 = bf16[1280,4096]{1,0:T(8,128)(2,1)} fusion(bf16[1024,4096]{1,0:T(8,128)(2,1)} %all-gather.2.cloned.1.call-done, s32[2048]{0:T(1024)S(1)} %pad_clamp_fusion), kind=kCustom, calls=%fused_computation.1 | custom fusion | bytes 20976640 | tf_op jit(solution)/shard_map/jit(_take)/gather | solution.py:53
  121.9 6.9 %multiply_reduce_fusion = f32[1280]{0:T(1024)S(1)} fusion(bf16[1280,4096]{1,0:T(8,128)(2,1)} %gather_fusion.1, pred[1280]{0:T(1024)(128)(4,1)S(1)} %get-tuple-element.5), kind=kLoop, calls=%fused_computation.9 | loop fusion | flops 20970240 | bytes 10492160 | tf_op jit(solution)/shard_map/reduce_sum | solution.py:54
  128.8 0.1 rsqrt.12
  128.9 0.0 copy-done
  128.9 9.0 %fusion.1 = bf16[16,80,4096]{2,1,0:T(8,128)(2,1)S(1)} fusion(f32[4096]{0:T(1024)S(1)} %copy-done, f32[16,80]{1,0:T(8,128)S(1)} %rsqrt.12, bf16[16,80,4096]{2,1,0:T(8,128)(2,1)} %bitcast.44, pred[16,80]{1,0:T(8,128)(4,1)S(1)} %broadcast_in_dim.109, pred[16,80]{1,0:T(8,128)(4,1)S(1)} %broadcast_in_dim.105), kind=kLoop, calls=%fused_computation.11 | loop fusion | flops 31457280 | bytes 20995584 | tf_op jit(solution)/shard_map/jit(_where)/select_n | solution.py:56
  138.0 0.0 slice-start
  138.0 0.0 slice-start.2
  138.0 123.9 %all_to_all.18 = bf16[16,80,4096]{2,1,0:T(8,128)(2,1)S(1)} all-to-all(bf16[16,80,4096]{2,1,0:T(8,128)(2,1)S(1)} %fusion.1), channel_id=1, replica_groups=mesh['rep'=16,'exp'=8] {'rep'}, dimensions={0} | all-to-all | bytes 20971520 | tf_op jit(solution)/shard_map/all_to_all | solution.py:57
  261.9 11.8 %fusion.7 = f32[1280,768]{1,0:T(8,128)} fusion(bf16[1280,4096]{1,0:T(8,128)(2,1)S(1)} %bitcast.46, bf16[1,4096,768]{2,1,0:T(8,128)(2,1)} %param.15), kind=kOutput, calls=%fused_computation.17 | convolution fusion | flops 8053063680 | bytes 20709376 | tf_op jit(solution)/shard_map/dot_general | solution.py:8
  273.7 0.0 slice-done
  273.7 0.0 slice-done.1
  273.7 10.3 %fusion.12 = bf16[1280,768]{1,0:T(8,128)(2,1)S(1)} fusion(bf16[1280,4096]{1,0:T(8,128)(2,1)S(1)} %bitcast.47, bf16[1,4096,768]{2,1,0:T(8,128)(2,1)S(1)} %bitcast.53, f32[1280,768]{1,0:T(8,128)} %fusion.7), kind=kOutput, calls=%fused_computation.20 | convolution fusion | flops 8058961920 | bytes 22675456 | tf_op jit(solution)/shard_map/dot_general | solution.py:9
  284.1 10.7 %convolution_convert_fusion = bf16[1280,4096]{1,0:T(8,128)(2,1)} fusion(bf16[1280,768]{1,0:T(8,128)(2,1)S(1)} %fusion.12, bf16[1,768,4096]{2,1,0:T(8,128)(2,1)S(1)} %bitcast.55), kind=kOutput, calls=%fused_computation.10 | convolution fusion | flops 8058306560 | bytes 18743296 | tf_op jit(solution)/shard_map/dot_general | solution.py:11
  294.7 5.0 all-to-all-start.1
  299.7 0.0 reduce-scatter.2.cloned.1.call-start
  299.8 14.9 %all_gather.10 = f32[1024,8]{0,1:T(8,128)S(1)} all-gather(f32[128,8]{0,1:T(8,128)S(1)} %divide_multiply_fusion), channel_id=1, replica_groups=mesh['rep'=16,'exp'=8] {'exp'}, dimensions={0}, use_global_device_ids=true | all-gather | bytes 36864 | tf_op jit(solution)/shard_map/all_gather | solution.py:41
  314.7 0.2 copy.35
  314.9 0.3 reshape.190
  315.1 30.4 %scatter_custom_fusion.2 = f32[1280]{0:T(1024)S(1)} fusion(s32[8192]{0:T(1024)S(1)} %bitcast.50, f32[8192]{0:T(1024)S(1)} %reshape.190, f32[]{:T(128)} %constant.89.clone.1), kind=kCustom, calls=%fused_computation.67 | custom fusion | bytes 5124 | tf_op jit(solution)/shard_map/scatter | solution.py:52
  345.6 126.3 %all-to-all-done.1 = bf16[16,80,4096]{2,1,0:T(8,128)(2,1)} async-done(((bf16[16,80,4096]{2,1,0:T(8,128)(2,1)}), bf16[16,80,4096]{2,1,0:T(8,128)(2,1)}, u32[]{:S(2)}, u32[]{:S(2)}) %all-to-all-start.1) | async-done | bytes 10485792 | tf_op jit(solution)/shard_map/all_to_all | solution.py:59
  471.9 42.9 %scatter_custom_fusion.3 = f32[1024,4096]{1,0:T(8,128)} fusion(s32[1280]{0:T(1024)S(1)} %get-tuple-element.8, bf16[1280,4096]{1,0:T(8,128)(2,1)} %bitcast.16, f32[1280]{0:T(1024)S(1)} %scatter_custom_fusion.2, f32[]{:T(128)} %constant.89.clone.1), kind=kCustom, calls=%fused_computation.7 | custom fusion | flops 15728640 | bytes 27271172 | tf_op jit(solution)/shard_map/scatter-add | solution.py:62
  514.8 9.0 %convert_element_type.50 = bf16[1024,4096]{1,0:T(8,128)(2,1)} convert(f32[1024,4096]{1,0:T(8,128)} %scatter_custom_fusion.3) | non-fusion elementwise | flops 4194304 | bytes 25165824 | tf_op jit(solution)/shard_map/convert_element_type | solution.py:63
  523.8 0.0 reduce-scatter.2.cloned.1.call-update
  523.8 59.5 %reduce-scatter.2.cloned.1.call-done = bf16[128,4096]{1,0:T(8,128)(2,1)} async-done(((bf16[1024,4096]{1,0:T(8,128)(2,1)}), bf16[128,4096]{1,0:T(8,128)(2,1)}) %reduce-scatter.2.cloned.1.call-update) | async-done | bytes 1048592 | tf_op jit(solution)/shard_map/reduce_scatter | solution.py:63
  (31 shorter events, 0.4 us)
Async XLA Ops:
  6.5 92.2 %all-gather.2.cloned.1.call-start = ((), (), s32[]{:S(2)}) async-start(), calls=%async_computation.3 | async-start | bytes 9437184 | tf_op jit(solution)/shard_map/all_gather | solution.py:39
  121.9 7.0 %copy-start = (f32[4096]{0:T(1024)S(1)}, f32[4096]{0:T(1024)}, u32[]{:S(2)}) copy-start(f32[4096]{0:T(1024)} %param.14) | copy-start | bytes 49156
  138.0 135.8 %slice-start = ((s8[6291456]{0:T(1024)(128)(4,1)}), s8[4194304]{0:T(1024)(128)(4,1)S(1)}, s32[]{:S(2)}) async-start(s8[6291456]{0:T(1024)(128)(4,1)} %bitcast.52), calls=%async_computation.5 | async-start | bytes 8388608
  138.0 146.1 %slice-start.2 = ((s8[6291456]{0:T(1024)(128)(4,1)}), s8[4194304]{0:T(1024)(128)(4,1)S(1)}, s32[]{:S(2)}) async-start(s8[6291456]{0:T(1024)(128)(4,1)} %bitcast.54), calls=%async_computation.7 | async-start | bytes 8388608
  261.9 11.8 %slice-start.1 = ((s8[6291456]{0:T(1024)(128)(4,1)}), s8[2097152]{0:T(1024)(128)(4,1)S(1)}, s32[]{:S(2)}) async-start(s8[6291456]{0:T(1024)(128)(4,1)} %bitcast.52), calls=%async_computation.6 | async-start | bytes 4194304
  261.9 22.2 %slice-start.3 = ((s8[6291456]{0:T(1024)(128)(4,1)}), s8[2097152]{0:T(1024)(128)(4,1)S(1)}, s32[]{:S(2)}) async-start(s8[6291456]{0:T(1024)(128)(4,1)} %bitcast.54), calls=%async_computation.8 | async-start | bytes 4194304
  294.7 5.0 copy-start.1
  294.7 177.1 %all-to-all-start.1 = ((bf16[16,80,4096]{2,1,0:T(8,128)(2,1)}), bf16[16,80,4096]{2,1,0:T(8,128)(2,1)}, u32[]{:S(2)}, u32[]{:S(2)}) async-start(bf16[16,80,4096]{2,1,0:T(8,128)(2,1)} %bitcast.45), calls=%async_computation.1 | async-start | bytes 20971520 | tf_op jit(solution)/shard_map/all_to_all | solution.py:59
  299.7 283.6 %reduce-scatter.2.cloned.1.call-start = ((), (), s32[]{:S(2)}) async-start(), calls=%async_computation.4 | async-start | bytes 9437184 | tf_op jit(solution)/shard_map/reduce_scatter | solution.py:63
Sparse Core Ops, SparseCore 0:
  9.1 53.5 all-gather.1
  523.9 59.3 reduce-scatter.1
where the time goes:
time: 597 us; the launch traced here: 590 us
  waiting for transfers between devices  187 us (31%)
  blocking collectives  154 us (26%)
  local copies, waits for them, and re-layouts  127 us (21%)
  other arithmetic  70.3 us (12%)
  matrix products  32.8 us (5%)
  between operations  14.6 us (2%)
    all_to_all x1, waiting for transfers between devices, shards(): lax.all_to_all(results, 'rep', split_axis=0, concat_axis=0, tiled=True)  126 us
    all_to_all x1, blocking collectives, shards(): lax.all_to_all(outgoing, 'rep', split_axis=0, concat_axis=0, tiled=True)  124 us
    reduce_scatter x1, waiting for transfers between devices, shards(): lax.psum_scatter(partial.astype(jnp.bfloat16), 'exp', scatter_dimension=0...  59.5 us
    scatter-add x1, other arithmetic, shards(): jnp.zeros((micro, width), jnp.float32).at[target].add(contrib, mode='drop')  42.9 us
    scatter x1, local copies, waits for them, and re-layouts, shards(): filled = jnp.zeros((slots,), jnp.bool_).at[dest].set(True, mode='drop')  34.6 us
    scatter x1, local copies, waits for them, and re-layouts, shards(): src_row = jnp.zeros((slots,), jnp.int32).at[dest].set(row_id, mode='drop')  30.9 us
    scatter x1, local copies, waits for them, and re-layouts, shards(): jnp.zeros((slots,), jnp.float32).at[dest]  30.4 us
    gather x1, local copies, waits for them, and re-layouts, shards(): jnp.take(group, jnp.take(parent_all, src_row), axis=0).astype(jnp.float32)  23.2 us
  transfers between devices with their start and end apart: 3, of which 2 were waited for; matrix products, arithmetic and copies ran while one was open for 18% of the time, Pallas kernels for 0%

commit v1 on v0

--- a/solution.py
+++ b/solution.py
@@ -38,7 +38,12 @@
     )
     group = lax.all_gather(hidden, "exp", axis=0, tiled=True)
     ints_all = lax.all_gather(ints, "exp", axis=0, tiled=True)
-    w_all = lax.all_gather(weights, "exp", axis=0, tiled=True)
+    ring = [weights]
+    for hop in range(7):
+        ring.append(lax.ppermute(ring[-1], "exp", [(dev, (dev + 1) % 8) for dev in range(8)]))
+    w_all = jnp.roll(
+        jnp.concatenate(ring[::-1], axis=0), (lax.axis_index("exp") + 1) * ring[0].shape[0], axis=0
+    )
     code_all = ints_all[:, :top]
     rank_all = ints_all[:, top : 2 * top]
     parent_all = ints_all[:, 2 * top]

time: 597 us -> 597 us (level)
  blocking collectives: 154 us -> 139 us
  starting transfers between devices: 5.02 us -> 14.3 us
    ppermute x0 -> x7, waiting for transfers between devices: none -> 19.2 us  [shards(): lax.ppermute(ring[-1], 'exp', [(dev, (dev + 1) % 8) for dev in range(8)])]
    all_gather x1 -> x0, blocking collectives: 14.9 us -> none  [shards(): w_all = lax.all_gather(weights, 'exp', axis=0, tiled=True)]
    all_to_all x1, waiting for transfers between devices: 126 us -> 112 us  [shards(): lax.all_to_all(results, 'rep', split_axis=0, concat_axis=0, tiled=True)]
    ppermute x0 -> x7, starting transfers between devices: none -> 9.23 us  [shards(): lax.ppermute(ring[-1], 'exp', [(dev, (dev + 1) % 8) for dev in range(8)])]
  transfers between devices with their start and end apart: 3 -> 10, of which waited for: 2 -> 9; matrix products, arithmetic and copies ran while one was open for 18% -> 18% of each run, Pallas kernels for 0% -> 0%
where the time goes in v1:
time: 597 us; the launch traced here: 590 us
  waiting for transfers between devices  192 us (32%)
  blocking collectives  139 us (23%)
  local copies, waits for them, and re-layouts  127 us (21%)
  other arithmetic  70.3 us (12%)
  matrix products  32.8 us (5%)
  between operations  14.7 us (2%)
  starting transfers between devices  14.3 us (2%)
    all_to_all x1, blocking collectives, shards(): lax.all_to_all(outgoing, 'rep', split_axis=0, concat_axis=0, tiled=True)  124 us
    all_to_all x1, waiting for transfers between devices, shards(): lax.all_to_all(results, 'rep', split_axis=0, concat_axis=0, tiled=True)  112 us
    reduce_scatter x1, waiting for transfers between devices, shards(): lax.psum_scatter(partial.astype(jnp.bfloat16), 'exp', scatter_dimension=0...  59.5 us
    scatter-add x1, other arithmetic, shards(): jnp.zeros((micro, width), jnp.float32).at[target].add(contrib, mode='drop')  42.9 us
    scatter x1, local copies, waits for them, and re-layouts, shards(): filled = jnp.zeros((slots,), jnp.bool_).at[dest].set(True, mode='drop')  34.6 us
    scatter x1, local copies, waits for them, and re-layouts, shards(): src_row = jnp.zeros((slots,), jnp.int32).at[dest].set(row_id, mode='drop')  30.9 us
    scatter x1, local copies, waits for them, and re-layouts, shards(): jnp.zeros((slots,), jnp.float32).at[dest]  30.4 us
    gather x1, local copies, waits for them, and re-layouts, shards(): jnp.take(group, jnp.take(parent_all, src_row), axis=0).astype(jnp.float32)  23.2 us
  transfers between devices with their start and end apart: 10, of which 9 were waited for; matrix products, arithmetic and copies ran while one was open for 18% of the time, Pallas kernels for 0%

profile of v1, /device:TPU:1, one launch (start us, length us, event | category | flops | bytes accessed | tf_op | source)
XLA Modules:
  0.0 590.2 jit_solution(5646565075315554811)
XLA Ops:
  6.5 0.7 all-gather.2.cloned.1.call-update
  7.3 0.8 copy.28
  8.0 0.1 eq.40
  8.1 0.1 eq.36
  8.9 0.1 broadcast_in_dim.94.clone
  9.0 0.1 and.61
  9.1 0.1 copy.31
  9.2 0.3 fusion.17
  9.7 0.1 copy.32
  9.8 0.5 fusion.16
  10.3 0.1 reshape.149
  10.4 0.7 broadcast_select_fusion
  11.1 0.7 pad_add_fusion
  11.8 15.3 %all_gather.6 = s32[1024,17]{0,1:T(8,128)S(1)} all-gather(s32[128,17]{0,1:T(8,128)S(1)} %pad_add_fusion), channel_id=1, replica_groups=mesh['rep'=16,'exp'=8] {'exp'}, dimensions={0}, use_global_device_ids=true | all-gather | bytes 78336 | tf_op jit(solution)/shard_map/all_gather | solution.py:40
  27.1 0.2 copy.34
  27.3 0.3 reshape.150
  27.7 34.6 %scatter_custom_fusion = pred[1280]{0:T(1024)(128)(4,1)S(1)} fusion(s32[8192]{0:T(1024)S(1)} %bitcast.48, pred[8192]{0:T(1024)(128)(4,1)S(1)} %broadcast.156, pred[]{:T(512)} %constant.109.clone.1), kind=kCustom, calls=%fused_computation.88 | custom fusion | bytes 1281 | tf_op jit(solution)/shard_map/scatter | solution.py:56
  62.3 0.1 broadcast_in_dim.105
  62.4 0.3 reshape.182
  62.7 30.9 %scatter_custom_fusion.1 = s32[1280]{0:T(1024)S(1)} fusion(s32[8192]{0:T(1024)S(1)} %bitcast.49, s32[8192]{0:T(1024)S(1)} %reshape.182, s32[]{:T(128)} %constant.112.clone.1), kind=kCustom, calls=%fused_computation.85 | custom fusion | bytes 5124 | tf_op jit(solution)/shard_map/scatter | solution.py:55
  93.6 5.0 gather_fusion
  98.6 0.1 broadcast_in_dim.109
  98.7 23.2 %gather_fusion.1 = bf16[1280,4096]{1,0:T(8,128)(2,1)} fusion(bf16[1024,4096]{1,0:T(8,128)(2,1)} %all-gather.2.cloned.1.call-done, s32[2048]{0:T(1024)S(1)} %pad_clamp_fusion), kind=kCustom, calls=%fused_computation.1 | custom fusion | bytes 20976640 | tf_op jit(solution)/shard_map/jit(_take)/gather | solution.py:58
  121.9 6.9 %multiply_reduce_fusion = f32[1280]{0:T(1024)S(1)} fusion(bf16[1280,4096]{1,0:T(8,128)(2,1)} %gather_fusion.1, pred[1280]{0:T(1024)(128)(4,1)S(1)} %get-tuple-element.5), kind=kLoop, calls=%fused_computation.9 | loop fusion | flops 20970240 | bytes 10492160 | tf_op jit(solution)/shard_map/reduce_sum | solution.py:59
  128.9 9.0 %fusion.1 = bf16[16,80,4096]{2,1,0:T(8,128)(2,1)S(1)} fusion(f32[4096]{0:T(1024)S(1)} %copy-done.1, f32[16,80]{1,0:T(8,128)S(1)} %rsqrt.12, bf16[16,80,4096]{2,1,0:T(8,128)(2,1)} %bitcast.44, pred[16,80]{1,0:T(8,128)(4,1)S(1)} %broadcast_in_dim.109, pred[16,80]{1,0:T(8,128)(4,1)S(1)} %broadcast_in_dim.105), kind=kLoop, calls=%fused_computation.11 | loop fusion | flops 31457280 | bytes 20995584 | tf_op jit(solution)/shard_map/jit(_where)/select_n | solution.py:61
  138.0 123.9 %all_to_all.18 = bf16[16,80,4096]{2,1,0:T(8,128)(2,1)S(1)} all-to-all(bf16[16,80,4096]{2,1,0:T(8,128)(2,1)S(1)} %fusion.1), channel_id=1, replica_groups=mesh['rep'=16,'exp'=8] {'rep'}, dimensions={0} | all-to-all | bytes 20971520 | tf_op jit(solution)/shard_map/all_to_all | solution.py:62
  261.9 11.8 %fusion.7 = f32[1280,768]{1,0:T(8,128)} fusion(bf16[1280,4096]{1,0:T(8,128)(2,1)S(1)} %bitcast.46, bf16[1,4096,768]{2,1,0:T(8,128)(2,1)} %param.15), kind=kOutput, calls=%fused_computation.17 | convolution fusion | flops 8053063680 | bytes 20709376 | tf_op jit(solution)/shard_map/dot_general | solution.py:8
  273.7 10.3 %fusion.12 = bf16[1280,768]{1,0:T(8,128)(2,1)S(1)} fusion(bf16[1280,4096]{1,0:T(8,128)(2,1)S(1)} %bitcast.47, bf16[1,4096,768]{2,1,0:T(8,128)(2,1)S(1)} %bitcast.53, f32[1280,768]{1,0:T(8,128)} %fusion.7), kind=kOutput, calls=%fused_computation.20 | convolution fusion | flops 8058961920 | bytes 22675456 | tf_op jit(solution)/shard_map/dot_general | solution.py:9
  284.1 10.7 %convolution_convert_fusion = bf16[1280,4096]{1,0:T(8,128)(2,1)} fusion(bf16[1280,768]{1,0:T(8,128)(2,1)S(1)} %fusion.12, bf16[1,768,4096]{2,1,0:T(8,128)(2,1)S(1)} %bitcast.55), kind=kOutput, calls=%fused_computation.10 | convolution fusion | flops 8058306560 | bytes 18743296 | tf_op jit(solution)/shard_map/dot_general | solution.py:11
  294.7 5.0 all-to-all-start.1
  299.8 3.5 collective-permute-start
  303.3 0.8 collective-permute-done
  304.1 2.3 collective-permute-start.1
  306.4 0.8 collective-permute-done.1
  307.1 2.3 collective-permute-start.2
  309.4 1.9 collective-permute-done.2
  311.2 1.2 collective-permute-start.3
  312.4 3.1 collective-permute-done.3
  315.5 4.2 collective-permute-done.4
  319.7 4.2 collective-permute-done.5
  324.0 4.2 collective-permute-done.6
  328.4 0.2 copy.35
  328.6 0.3 reshape.190
  328.8 30.4 %scatter_custom_fusion.2 = f32[1280]{0:T(1024)S(1)} fusion(s32[8192]{0:T(1024)S(1)} %bitcast.50, f32[8192]{0:T(1024)S(1)} %reshape.190, f32[]{:T(128)} %constant.108.clone.1), kind=kCustom, calls=%fused_computation.83 | custom fusion | bytes 5124 | tf_op jit(solution)/shard_map/scatter | solution.py:57
  359.3 112.4 %all-to-all-done.1 = bf16[16,80,4096]{2,1,0:T(8,128)(2,1)} async-done(((bf16[16,80,4096]{2,1,0:T(8,128)(2,1)}), bf16[16,80,4096]{2,1,0:T(8,128)(2,1)}, u32[]{:S(2)}, u32[]{:S(2)}) %all-to-all-start.1) | async-done | bytes 10485792 | tf_op jit(solution)/shard_map/all_to_all | solution.py:64
  471.7 42.9 %scatter_custom_fusion.3 = f32[1024,4096]{1,0:T(8,128)} fusion(s32[1280]{0:T(1024)S(1)} %get-tuple-element.8, bf16[1280,4096]{1,0:T(8,128)(2,1)} %bitcast.16, f32[1280]{0:T(1024)S(1)} %scatter_custom_fusion.2, f32[]{:T(128)} %constant.108.clone.1), kind=kCustom, calls=%fused_computation.7 | custom fusion | flops 15728640 | bytes 27271172 | tf_op jit(solution)/shard_map/scatter-add | solution.py:67
  514.6 9.0 %convert_element_type.50 = bf16[1024,4096]{1,0:T(8,128)(2,1)} convert(f32[1024,4096]{1,0:T(8,128)} %scatter_custom_fusion.3) | non-fusion elementwise | flops 4194304 | bytes 25165824 | tf_op jit(solution)/shard_map/convert_element_type | solution.py:68
  523.6 59.5 %reduce-scatter.2.cloned.1.call-done = bf16[128,4096]{1,0:T(8,128)(2,1)} async-done(((bf16[1024,4096]{1,0:T(8,128)(2,1)}), bf16[128,4096]{1,0:T(8,128)(2,1)}) %reduce-scatter.2.cloned.1.call-update) | async-done | bytes 1048592 | tf_op jit(solution)/shard_map/reduce_scatter | solution.py:68
  (61 shorter events, 0.6 us)
Async XLA Ops:
  6.5 92.2 %all-gather.2.cloned.1.call-start = ((), (), s32[]{:S(2)}) async-start(), calls=%async_computation.3 | async-start | bytes 9437184 | tf_op jit(solution)/shard_map/all_gather | solution.py:39
  121.9 7.0 %copy-start.1 = (f32[4096]{0:T(1024)S(1)}, f32[4096]{0:T(1024)}, u32[]{:S(2)}) copy-start(f32[4096]{0:T(1024)} %param.14) | copy-start | bytes 49156
  138.0 135.8 %slice-start = ((s8[6291456]{0:T(1024)(128)(4,1)}), s8[4194304]{0:T(1024)(128)(4,1)S(1)}, s32[]{:S(2)}) async-start(s8[6291456]{0:T(1024)(128)(4,1)} %bitcast.52), calls=%async_computation.5 | async-start | bytes 8388608
  138.0 146.1 %slice-start.2 = ((s8[6291456]{0:T(1024)(128)(4,1)}), s8[4194304]{0:T(1024)(128)(4,1)S(1)}, s32[]{:S(2)}) async-start(s8[6291456]{0:T(1024)(128)(4,1)} %bitcast.54), calls=%async_computation.7 | async-start | bytes 8388608
  261.9 11.8 %slice-start.1 = ((s8[6291456]{0:T(1024)(128)(4,1)}), s8[2097152]{0:T(1024)(128)(4,1)S(1)}, s32[]{:S(2)}) async-start(s8[6291456]{0:T(1024)(128)(4,1)} %bitcast.52), calls=%async_computation.6 | async-start | bytes 4194304
  261.9 22.1 %slice-start.3 = ((s8[6291456]{0:T(1024)(128)(4,1)}), s8[2097152]{0:T(1024)(128)(4,1)S(1)}, s32[]{:S(2)}) async-start(s8[6291456]{0:T(1024)(128)(4,1)} %bitcast.54), calls=%async_computation.8 | async-start | bytes 4194304
  294.7 5.1 copy-start
  294.7 176.9 %all-to-all-start.1 = ((bf16[16,80,4096]{2,1,0:T(8,128)(2,1)}), bf16[16,80,4096]{2,1,0:T(8,128)(2,1)}, u32[]{:S(2)}, u32[]{:S(2)}) async-start(bf16[16,80,4096]{2,1,0:T(8,128)(2,1)} %bitcast.45), calls=%async_computation.1 | async-start | bytes 20971520 | tf_op jit(solution)/shard_map/all_to_all | solution.py:64
  299.7 283.4 %reduce-scatter.2.cloned.1.call-start = ((), (), s32[]{:S(2)}) async-start(), calls=%async_computation.4 | async-start | bytes 9437184 | tf_op jit(solution)/shard_map/reduce_scatter | solution.py:68
  299.8 4.2 collective-permute-start
  304.1 3.0 collective-permute-start.1
  307.1 4.1 collective-permute-start.2
  311.2 4.2 collective-permute-start.3
  315.5 4.2 collective-permute-start.4
  319.7 4.2 collective-permute-start.5
  324.0 4.2 collective-permute-start.6
Sparse Core Ops, SparseCore 0:
  9.1 53.5 all-gather.1
  523.7 59.3 reduce-scatter.1
